TPU v7x, 256 devices: a whole 4x4x8 slice. The times are simulated.
256 devices in a mesh: order: 16 (over x_hi, z), blk: 16 (over y, x_lo, core).
Axes of the slice: x: 4 (x_hi: 2, x_lo: 2; x = x_hi * 2 + x_lo), y: 4, z: 8, core: 2. Of those that a mesh axis runs over, the one named last changes fastest.
Arguments:
- fourier_cycles: float32 [32, 512, 128], P('order', 'blk'), parts along dimension 0, may hold values from -6 to 6
- legendre: float32 [32, 512, 12288], P('order', 'blk'), parts along dimension 0, may hold values from -0.25 to 0.25
- cycle_weight: float32 [512], P('blk'), may hold values from 0.5 to 2
- matched_filter_weights: float32 [12288, 8, 8], P('blk'), may hold values from -2 to 2
- cluster_cycles: int32 [32, 64], P('order'), parts along dimension 0, may hold values from 0 to 511
- cluster_flux: float32 [32, 64, 128], P('order'), parts along dimension 0, may hold values from -18 to 18
- order_per_slot: int32 [32], P('order'), parts along dimension 0, may hold values from 0 to 6143
Outputs:
- synthesized: float32 [32, 512, 128], P('order', 'blk'), parts along dimension 0
There are 16 independent parts, one for each index of `order`. A program takes and returns all parts, laid end to end along the dimension named above; an argument that names none is the same for every part. Nothing has to cross between parts.
Inputs may be any that keep to these rules, and one draw needn't show every extreme that they name: `cluster_cycles`: cycle indices; several clusters may share a cycle, and their coefficients add. `order_per_slot`: order of each slot; degrees below it carry no coefficients.
All inputs are finite; a program needn't handle non-finite values.
Results may differ from a plain program's by a relative error of at most 0.00011.
Values sent between devices are 32-bit elements; how exact they have to be, the bound alone decides.
A program may use at most 128 MiB of HBM per device.

v0:
```python
import jax
import jax.numpy as jnp
from jax import lax
from jax.sharding import PartitionSpec as P

L = 12288
F = 8
S = 8
SIMS = 8
M = 2


highest_degree = lax.Precision.HIGHEST


def inject(fourier_cycles, cycle_weight, cluster_cycles, cluster_flux):
    local = fourier_cycles.shape[1]
    cycle_ids = lax.axis_index("blk") * local + lax.iota(jnp.int32, local)
    cycle_hits = (cycle_ids[None, :, None] == cluster_cycles[:, None, :]).astype(jnp.float32)
    added = jnp.einsum("krj,kjc->krc", cycle_hits, cluster_flux, precision=highest_degree)
    return cycle_weight[None, :, None] * (fourier_cycles + added)


def finish(owned, matched_filter_weights, order_per_slot):
    blocks = owned.shape[0]
    degrees = lax.axis_index("blk") * blocks + lax.iota(jnp.int32, blocks)
    harmonics = owned.reshape(blocks, M, 2 * F * SIMS)
    kept_mask = (degrees[:, None] >= order_per_slot[None, :]).astype(jnp.float32)
    masked_values = (harmonics * kept_mask[:, :, None]).reshape(blocks, M, 2, F, SIMS)
    matched_output = jnp.einsum(
        "dvr,dotrq->dotvq", matched_filter_weights, masked_values, precision=highest_degree
    )
    squares = jnp.sum(matched_filter_weights * matched_filter_weights, axis=2)
    weights = kept_mask * (2.0 * degrees.astype(jnp.float32) + 1.0)[:, None]
    response = jnp.einsum("lk,ls->ks", weights, squares, precision=highest_degree)
    response = lax.psum(response, "blk")
    scaled = matched_output * (L / jnp.sqrt(response))[None, :, None, :, None]
    return scaled.reshape(blocks, M, 2 * S * SIMS)


def body(
    fourier_cycles,
    legendre,
    cycle_weight,
    matched_filter_weights,
    cluster_cycles,
    cluster_flux,
    order_per_slot,
):
    injected = inject(fourier_cycles, cycle_weight, cluster_cycles, cluster_flux)
    orders_here = legendre.shape[0]
    width = injected.shape[2]
    blocks = legendre.shape[2] // lax.axis_size("blk")
    columns = legendre
    partial_running_sum = jnp.einsum("krl,krc->lkc", columns, injected, precision=highest_degree)
    owned = lax.psum_scatter(
        partial_running_sum.reshape(blocks * lax.axis_size("blk"), orders_here * width),
        "blk",
        scatter_dimension=0,
        tiled=True,
    )
    scaled = finish(owned, matched_filter_weights, order_per_slot)
    columns = legendre
    return jnp.einsum(
        "krl,lkc->krc",
        columns,
        lax.all_gather(scaled, "blk", axis=0, tiled=True),
        precision=highest_degree,
    )


def solution(mesh):
    return jax.shard_map(
        body,
        mesh=mesh,
        in_specs=(
            P("order", "blk", None),
            P("order", "blk", None),
            P("blk"),
            P("blk", None, None),
            P("order", None),
            P("order", None, None),
            P("order"),
        ),
        out_specs=P("order", "blk", None),
        check_vma=False,
    )
```

profile of v0, /device:TPU:1, one launch (start us, length us, event | category | flops | bytes accessed | tf_op | source)
XLA Modules:
  0.0 300.5 jit_solution(4388038787292911202)
XLA Ops:
  6.5 0.0 copy-start
  6.5 0.0 reduce-scatter.2.cloned.1.call-start
  6.5 1.2 fusion
  7.7 0.8 copy-done
  8.5 0.0 copy-start.1
  8.5 12.6 %fusion.10 = f32[2,128,12288]{2,1,0:T(8,128)} fusion(f32[2,32,128]{2,1,0:T(8,128)S(1)} %fusion, f32[2,32,12288]{2,1,0:T(8,128)S(1)} %copy-done), kind=kOutput, calls=%fused_computation.21 | convolution fusion | flops 1207959552 | bytes 15761408 | tf_op jit(solution)/shard_map/krl,krc->lkc/dot_general | solution.py:55
  21.1 0.0 reduce-scatter.2.cloned.1.call-update
  21.1 0.0 all-gather.2.cloned.1.call-start
  21.1 0.0 copy-done.1
  21.2 2.3 copy.17
  23.5 0.1 multiply_reduce_fusion
  23.5 0.0 copy-done.2
  23.5 0.2 fusion.4
  23.7 30.7 %psum.7 = f32[2,8]{1,0:T(2,128)S(1)} all-reduce(f32[2,8]{1,0:T(2,128)S(1)} %fusion.4), channel_id=1, replica_groups=mesh['order'=16,'blk'=16] {'blk'}, use_global_device_ids=true, to_apply=%region_2.0 | all-reduce | flops 16 | bytes 128 | tf_op jit(solution)/shard_map/psum | solution.py:36
  54.5 0.1 compare_convert_fusion
  54.5 111.8 %reduce-scatter.2.cloned.1.call-done = f32[768,256]{0,1:T(8,128)} async-done(((f32[12288,256]{0,1:T(8,128)}), f32[768,256]{0,1:T(8,128)}) %reduce-scatter.2.cloned.1.call-update) | async-done | bytes 786448 | tf_op jit(solution)/shard_map/reduce_scatter | solution.py:56
  166.3 2.1 broadcast_multiply_fusion
  168.4 11.3 %copy.13 = f32[768,2,2,8,8]{3,4,2,1,0:T(8,128)} copy(f32[768,2,2,8,8]{0,4,3,2,1:T(8,128)} %broadcast_multiply_fusion) | data formatting | bytes 1572864 | tf_op jit(solution)/shard_map/mul | solution.py:29
  179.8 16.1 %multiply_bitcast_fusion = f32[768,2,2,8,8]{3,4,2,1,0:T(8,128)} fusion(f32[2,8]{1,0:T(2,128)S(1)} %rsqrt_multiply_fusion, f32[768,2,2,8,8]{3,4,2,1,0:T(8,128)} %copy.13, f32[768,8,8,1,1]{2,1,4,3,0:T(8,128)} %copy.17), kind=kOutput, calls=%fused_computation | convolution fusion | flops 19070976 | bytes 1769536 | tf_op jit(solution)/shard_map/dvr,dotrq->dotvq/dot_general | solution.py:30
  195.8 9.9 %copy.15 = f32[768,2,2,8,8]{0,4,3,2,1:T(8,128)} copy(f32[768,2,2,8,8]{3,4,2,1,0:T(8,128)} %multiply_bitcast_fusion) | data formatting | bytes 1572864 | tf_op jit(solution)/shard_map/mul | solution.py:37
  205.8 2.3 copy.16
  208.1 0.0 all-gather.2.cloned.1.call-update
  208.1 75.4 %all-gather.2.cloned.1.call-done = f32[12288,2,128]{2,0,1:T(8,128)} async-done(((f32[768,2,128]{2,0,1:T(8,128)}), f32[12288,2,128]{2,0,1:T(8,128)}) %all-gather.2.cloned.1.call-update) | async-done | bytes 12582928 | tf_op jit(solution)/shard_map/all_gather | solution.py:67
  283.5 10.2 %convolution_bitcast_fusion = f32[2,32,128]{2,1,0:T(8,128)} fusion(f32[12288,2,128]{2,0,1:T(8,128)} %all-gather.2.cloned.1.call-done, f32[2,32,12288]{2,1,0:T(8,128)S(1)} %copy-done), kind=kOutput, calls=%fused_computation.1 | convolution fusion | flops 1207959552 | bytes 15761408 | tf_op jit(solution)/shard_map/krl,lkc->krc/dot_general | solution.py:64
  (5 shorter events, 0.0 us)
Async XLA Ops:
  6.5 2.0 copy-start
  6.5 159.8 %reduce-scatter.2.cloned.1.call-start = ((), (), s32[]{:S(2)}) async-start(), calls=%async_computation.1 | async-start | bytes 13369344 | tf_op jit(solution)/shard_map/reduce_scatter | solution.py:56
  8.5 12.6 %copy-start.1 = (f32[768,8,8]{0,2,1:T(8,128)S(1)}, f32[768,8,8]{0,2,1:T(8,128)}, u32[]{:S(2)}) copy-start(f32[768,8,8]{0,2,1:T(8,128)} %param.10) | copy-start | bytes 589828
  8.5 15.0 %copy-start.2 = (s32[2]{0:T(128)S(1)}, s32[2]{0:T(128)}, u32[]{:S(2)}) copy-start(s32[2]{0:T(128)} %param.13) | copy-start | bytes 28
  21.1 262.4 %all-gather.2.cloned.1.call-start = ((), (), s32[]{:S(2)}) async-start(), calls=%async_computation.2 | async-start | bytes 13369344 | tf_op jit(solution)/shard_map/all_gather | solution.py:67
Sparse Core Ops, SparseCore 0:
  21.2 145.0 reduce-scatter.1
  208.2 75.2 all-gather.1
where the time goes:
time: 301 us
  waiting for transfers between devices  187 us (62%)
  matrix products  40.3 us (13%)
  blocking collectives  30.7 us (10%)
  local copies, waits for them, and re-layouts  26.6 us (9%)
  between operations  13.4 us (4%)
    reduce_scatter x1, waiting for transfers between devices, body(): lax.psum_scatter(partial_running_sum.reshape(blocks * lax.axis_size('blk'...  112 us
    all_gather x1, waiting for transfers between devices, body(): lax.all_gather(scaled, 'blk', axis=0, tiled=True)  75.4 us
    psum x1, blocking collectives, finish(): response = lax.psum(response, 'blk')  30.7 us
    dot_general x1, matrix products, finish(): jnp.einsum('dvr,dotrq->dotvq', matched_filter_weights, masked_values, pre...  16.1 us
    dot_general x1, matrix products, body(): jnp.einsum('krl,krc->lkc', columns, injected, precision=highest_degree)  12.6 us
    mul x1, local copies, waits for them, and re-layouts, finish(): harmonics * kept_mask[:, :, None]  11.3 us
    dot_general x1, matrix products, body(): jnp.einsum('krl,lkc->krc', columns, lax.all_gather(scaled, 'blk', axis=0,...  10.2 us
    mul x1, local copies, waits for them, and re-layouts, finish(): scaled = matched_output * (L / jnp.sqrt(response))[None, :, None, :, None]  9.92 us
  transfers between devices with their start and end apart: 2, of which 2 were waited for; matrix products, arithmetic and copies ran while one was open for 1% of the time, Pallas kernels for 0%

commit v1 on v0

v1 whole, which is shorter than its diff:
```python
import functools

import jax
import jax.numpy as jnp
from jax import lax
from jax.experimental import pallas as pl
from jax.experimental.pallas import tpu as pltpu
from jax.sharding import PartitionSpec as P

L = 12288
F = 8
S = 8
SIMS = 8
M = 2
Y, X, CORES = 4, 2, 2
CHIPS = Y * X
N = CHIPS * CORES
CHUNKS = 3

MESH = pl.DeviceIdType.MESH
F32 = jnp.float32
BF16 = jnp.bfloat16

STEPS = [(dy, dx, dc) for dy in (1, 3, 2, 0) for dx in (0, 1) for dc in (0, 1) if (dy, dx, dc) != (0, 0, 0)]
CHIP_STEPS = [(dy, dx) for dy, dx, dc in STEPS if dc == 0]


def halves(value):
    high = value.astype(BF16)
    return high, (value - high.astype(F32)).astype(BF16)


def dot(a, b, dims=((1,), (0,))):
    return lax.dot_general(a, b, (dims, ((), ())), preferred_element_type=F32)


def kernel(
    cycles_hbm, legendre_hbm, weight_hbm, filter_hbm, hit_hbm, flux_hbm, order_ref, out_ref,
    own_cycles, own_weight, filters, hits, flux, load_sem,
    injected, injected_t, inj_send, inj_recv, pair_sem,
    responses, resp_send, resp_recv,
    blocks, block_send, block_recv, own_sem,
    high, low, harmonics, matched, total, from_core, core_sem, outgoing, arriving, sum_send, sum_recv,
):
    me = lax.axis_index("blk")
    y, x, core = me // (X * CORES), (me // CORES) % X, me % CORES
    chip = me // CORES
    rows = own_cycles.shape[1]
    half = CHIPS * rows
    degrees = filters.shape[2]
    wide = degrees // CHUNKS

    def chip_at(dy, dx):
        return ((y + dy) % Y) * X + (x + dx) % X

    def at(dy, dx, dc):
        return {"blk": chip_at(dy, dx) * CORES + (core + dc) % CORES}

    barrier = pltpu.get_barrier_semaphore()
    for step in STEPS:
        pl.semaphore_signal(barrier, inc=1, device_id=at(*step), device_id_type=MESH)

    loads = [
        pltpu.make_async_copy(source, target, load_sem.at[i])
        for i, (source, target) in enumerate(
            ((cycles_hbm, own_cycles), (weight_hbm, own_weight), (hit_hbm, hits), (flux_hbm, flux), (filter_hbm, filters))
        )
    ]
    for load in loads:
        load.start()

    own_rows = pl.ds(pl.multiple_of(half + chip * rows, rows), rows)

    def own_copy(j):
        return pltpu.make_async_copy(
            legendre_hbm.at[:, :, pl.ds(pl.multiple_of(me * degrees + j * wide, wide), wide)],
            blocks.at[j, :, own_rows, :],
            own_sem.at[j],
        )

    for j in range(CHUNKS):
        own_copy(j).start()
    for load in loads[:4]:
        load.wait()

    row = lax.broadcasted_iota(jnp.int32, (rows, rows), 0)
    lane = lax.broadcasted_iota(jnp.int32, (rows, rows), 1)
    weight = jnp.sum(jnp.where(row == lane, own_weight[...], 0.0), axis=1, keepdims=True)
    for k in range(M):
        clusters = hits.shape[1]
        cycle = me * rows + lax.broadcasted_iota(jnp.int32, (rows, clusters), 0)
        hit = (cycle == hits[k : k + 1, :]).astype(F32)
        added = lax.dot_general(
            hit, flux[k], (((1,), (0,)), ((), ())), precision=lax.Precision.HIGHEST, preferred_element_type=F32
        )
        injected[k, own_rows, :] = weight * (own_cycles[k] + added)

    loads[4].wait()
    degree = me * degrees + lax.broadcasted_iota(jnp.int32, (1, degrees), 1)
    squares = jnp.sum(filters[...] * filters[...], axis=1)
    scale_of = (lax.broadcasted_iota(jnp.int32, (S, 128), 1) // SIMS) % S == lax.broadcasted_iota(jnp.int32, (S, 128), 0)
    for k in range(M):
        factor = jnp.where(degree >= order_ref[k], 2.0 * degree.astype(F32) + 1.0, 0.0)
        response = jnp.sum(squares * factor, axis=1, keepdims=True)
        responses[me, k : k + 1, :] = jnp.sum(jnp.where(scale_of, response, 0.0), axis=0, keepdims=True)

    pl.semaphore_wait(barrier, N - 1)

    inj_copies = [
        pltpu.make_async_remote_copy(
            src_ref=injected.at[:, own_rows, :],
            dst_ref=injected.at[:, own_rows, :],
            send_sem=inj_send.at[i],
            recv_sem=inj_recv.at[i],
            device_id=at(dy, dx, 0),
            device_id_type=MESH,
        )
        for i, (dy, dx) in enumerate(CHIP_STEPS)
    ]
    for copy in inj_copies:
        copy.start()
    resp_copies = [
        pltpu.make_async_remote_copy(
            src_ref=responses.at[me],
            dst_ref=responses.at[me],
            send_sem=resp_send.at[i],
            recv_sem=resp_recv.at[i],
            device_id=at(*step),
            device_id_type=MESH,
        )
        for i, step in enumerate(STEPS)
    ]
    for copy in resp_copies:
        copy.start()

    def block_copy(j, i):
        dy, dx, dc = STEPS[i]
        there = chip_at(dy, dx) * CORES + (core + dc) % CORES
        return pltpu.make_async_remote_copy(
            src_ref=legendre_hbm.at[:, :, pl.ds(pl.multiple_of(there * degrees + j * wide, wide), wide)],
            dst_ref=blocks.at[j, :, pl.ds(pl.multiple_of((1 - dc) * half + chip * rows, rows), rows), :],
            send_sem=block_send.at[j, i],
            recv_sem=block_recv.at[j, i],
            device_id={"blk": there},
            device_id_type=MESH,
        )

    for j in range(CHUNKS):
        for i in range(N - 1):
            block_copy(j, i).start()

    for copy in inj_copies:
        copy.wait_recv()
    pair = pltpu.make_async_remote_copy(
        src_ref=injected.at[:, pl.ds(half, half), :],
        dst_ref=injected.at[:, pl.ds(0, half), :],
        send_sem=pair_sem.at[0],
        recv_sem=pair_sem.at[1],
        device_id=at(0, 0, 1),
        device_id_type=MESH,
    )
    pair.start()
    pair.wait_recv()
    for k in range(M):
        turned = jnp.transpose(injected[k])
        turned_high, turned_low = halves(turned)
        injected_t[k, 0:128, :] = turned_high
        injected_t[k, 128:256, :] = turned_low

    total[...] = jnp.zeros_like(total)
    core_copy = pltpu.make_async_remote_copy(
        src_ref=total.at[:, pl.ds(0, half), :],
        dst_ref=from_core,
        send_sem=core_sem.at[0],
        recv_sem=core_sem.at[1],
        device_id=at(0, 0, 1),
        device_id_type=MESH,
    )

    def chunk(j, carry):
        own_copy(j).wait()
        for i in range(N - 1):
            block_copy(j, i).wait_recv()
        start = pl.multiple_of(j * wide, wide)
        degree = me * degrees + j * wide + lax.broadcasted_iota(jnp.int32, (1, wide), 1)
        for k in range(M):
            block_high, block_low = halves(blocks[j, k])
            high[k] = block_high
            low[k] = block_low
            first = dot(injected_t[k], high[k])
            second = dot(injected_t[k, 0:128], low[k])
            value = first[0:128] + first[128:256] + second
            harmonics[k] = jnp.where(degree >= order_ref[k], value, 0.0)
            for t in range(wide // 128):
                lanes = pl.ds(t * 128, 128)
                for s in range(S):
                    sums = [None, None]
                    for f in range(F):
                        row = filters[s, f : f + 1, pl.ds(start + t * 128, 128)]
                        for p in range(2):
                            term = row * harmonics[k, pl.ds((p * F + f) * SIMS, SIMS), lanes]
                            sums[p] = term if f == 0 else sums[p] + term
                    for p in range(2):
                        out_high, out_low = halves(sums[p])
                        matched[k, pl.ds((p * S + s) * SIMS, SIMS), lanes] = out_high
                        matched[k, pl.ds(128 + (p * S + s) * SIMS, SIMS), lanes] = out_low
        for part in range(2):
            span = pl.ds(part * half, half)
            for k in range(M):
                both = dot(high[k, span, :], matched[k], ((1,), (1,)))
                third = dot(low[k, span, :], matched[k, 0:128], ((1,), (1,)))
                total[k, span, :] += both[:, 0:128] + both[:, 128:256] + third
            if part == 0:

                @pl.when(j == CHUNKS - 1)
                def _():
                    core_copy.start()

        return carry

    lax.fori_loop(0, CHUNKS, chunk, 0)

    for copy in resp_copies:
        copy.wait_recv()
    scale = L / jnp.sqrt(jnp.sum(responses[...], axis=0))
    core_copy.wait_recv()
    sum_copies = []
    for i, (dy, dx) in enumerate(CHIP_STEPS):
        there = chip_at(dy, dx) * rows
        outgoing[i] = (
            total[:, pl.ds(pl.multiple_of(half + there, rows), rows), :]
            + from_core[:, pl.ds(pl.multiple_of(there, rows), rows), :]
        )
        sum_copies.append(
            pltpu.make_async_remote_copy(
                src_ref=outgoing.at[i],
                dst_ref=arriving.at[i],
                send_sem=sum_send.at[i],
                recv_sem=sum_recv.at[i],
                device_id=at(dy, dx, 0),
                device_id_type=MESH,
            )
        )
    kept = total[:, own_rows, :] + from_core[:, pl.ds(pl.multiple_of(chip * rows, rows), rows), :]
    for copy in sum_copies:
        copy.start()
    for i, copy in enumerate(sum_copies):
        copy.wait_recv()
        kept = kept + arriving[i]
    out_ref[...] = kept * scale[:, None, :]

    for copy in inj_copies + resp_copies + [pair, core_copy] + sum_copies:
        copy.wait_send()
    for j in range(CHUNKS):
        for i in range(N - 1):
            block_copy(j, i).wait_send()


def body(cycles, legendre, weight, filters, hits, flux, order):
    orders, rows, width = cycles.shape
    degrees = filters.shape[0]
    clusters = hits.shape[1]
    wide = degrees // CHUNKS
    everyone = N * rows
    dma = pltpu.SemaphoreType.DMA
    anywhere = pl.BlockSpec(memory_space=pl.ANY)
    return pl.pallas_call(
        kernel,
        out_shape=jax.ShapeDtypeStruct(cycles.shape, F32),
        in_specs=[anywhere] * 6 + [pl.BlockSpec(memory_space=pltpu.SMEM)],
        out_specs=pl.BlockSpec(memory_space=pltpu.VMEM),
        scratch_shapes=[
            pltpu.VMEM((orders, rows, width), F32),
            pltpu.VMEM((1, rows), F32),
            pltpu.VMEM((S, F, degrees), F32),
            pltpu.VMEM((orders, clusters), jnp.int32),
            pltpu.VMEM((orders, clusters, width), F32),
            dma((5,)),
            pltpu.VMEM((orders, everyone, width), F32),
            pltpu.VMEM((orders, 2 * width, everyone), BF16),
            dma((CHIPS - 1,)),
            dma((CHIPS - 1,)),
            dma((2,)),
            pltpu.VMEM((N, orders, width), F32),
            dma((N - 1,)),
            dma((N - 1,)),
            pltpu.VMEM((CHUNKS, orders, everyone, wide), F32),
            dma((CHUNKS, N - 1)),
            dma((CHUNKS, N - 1)),
            dma((CHUNKS,)),
            pltpu.VMEM((orders, everyone, wide), BF16),
            pltpu.VMEM((orders, everyone, wide), BF16),
            pltpu.VMEM((orders, width, wide), F32),
            pltpu.VMEM((orders, 2 * width, wide), BF16),
            pltpu.VMEM((orders, everyone, width), F32),
            pltpu.VMEM((orders, everyone // 2, width), F32),
            dma((2,)),
            pltpu.VMEM((CHIPS - 1, orders, rows, width), F32),
            pltpu.VMEM((CHIPS - 1, orders, rows, width), F32),
            dma((CHIPS - 1,)),
            dma((CHIPS - 1,)),
        ],
        compiler_params=pltpu.CompilerParams(
            collective_id=0, has_side_effects=True, vmem_limit_bytes=60 * 1024 * 1024
        ),
    )(cycles, legendre, weight.reshape(1, rows), jnp.transpose(filters, (1, 2, 0)), hits, flux, order)


def solution(mesh):
    return jax.shard_map(
        body,
        mesh=mesh,
        in_specs=(
            P("order", "blk", None),
            P("order", "blk", None),
            P("blk"),
            P("blk", None, None),
            P("order", None),
            P("order", None, None),
            P("order"),
        ),
        out_specs=P("order", "blk", None),
        check_vma=False,
    )
```

time: 301 us -> 56.3 us (0.19)
  waiting for transfers between devices: 187 us -> 0 us
  Pallas kernels: 0 us -> 54.7 us
  matrix products: 40.3 us -> 0 us
  blocking collectives: 30.7 us -> 0 us
  local copies, waits for them, and re-layouts: 26.6 us -> 1.38 us
  between operations: 13.4 us -> 0.01 us
    reduce_scatter x1 -> x0, waiting for transfers between devices: 112 us -> none  [body(): lax.psum_scatter(partial_running_sum.reshape(blocks * lax.axis_size('blk'...]
    all_gather x1 -> x0, waiting for transfers between devices: 75.4 us -> none  [body(): lax.all_gather(scaled, 'blk', axis=0, tiled=True)]
    pallas_call x0 -> x1, Pallas kernels: none -> 54.7 us  [body(): pl.pallas_call(kernel, out_shape=jax.ShapeDtypeStruct(cycles.shape, F32),...]
    dot_general x5 -> x0, matrix products: 40.3 us -> none  [the longest x1 16.1 us: finish(): jnp.einsum('dvr,dotrq->dotvq', matched_filter_weights, masked_values, pre...]
    psum x1 -> x0, blocking collectives: 30.7 us -> none  [finish(): response = lax.psum(response, 'blk')]
    mul x2 -> x0, local copies, waits for them, and re-layouts: 21.3 us -> none  [the longest x1 11.3 us: finish(): harmonics * kept_mask[:, :, None]]
  transfers between devices with their start and end apart: 2 -> 0, of which waited for: 2 -> 0; matrix products, arithmetic and copies ran while one was open for 1% -> 0% of each run, Pallas kernels for 0% -> 0%
where the time goes in v1:
time: 56.3 us; the launch traced here: 56.1 us
  Pallas kernels  54.7 us (97%)
  local copies, waits for them, and re-layouts  1.38 us (2%)
    pallas_call x1, Pallas kernels, body(): pl.pallas_call(kernel, out_shape=jax.ShapeDtypeStruct(cycles.shape, F32),...  54.7 us
    unnamed x1, local copies, waits for them, and re-layouts  1.38 us

profile of v1, /device:TPU:1, one launch (start us, length us, event | category | flops | bytes accessed | tf_op | source)
XLA Modules:
  0.0 56.1 jit_solution(8225731063253497383)
XLA Ops:
  0.0 54.7 %shard_map.73 = f32[2,32,128]{2,1,0:T(8,128)} custom-call(f32[2,32,128]{2,1,0:T(8,128)} %cycles_hbm.1, f32[2,32,12288]{2,1,0:T(8,128)} %legendre_hbm.1, f32[1,32]{1,0:T(1,128)} %bitcast.3, f32[8,8,768]{2,1,0:T(8,128)} %bitcast.2, s32[2,64]{1,0:T(2,128)} %hit_hbm.1, f32[2,64,128]{2,1,0:T(8,128)} %flux_hbm.1, s32[2]{0:T(128)} %order_ref.1), custom_call_target="tpu_custom_call" | custom-call | tf_op jit(solution)/shard_map/pallas_call | solution.py:267
  54.7 1.4 %copy.9 = f32[2,32,128]{2,1,0:T(8,128)} copy(f32[2,32,128]{2,1,0:T(8,128)} %shard_map.73) | data formatting | bytes 65536

commit v2 on v1

v2 whole, which is shorter than its diff:
```python
import functools

import jax
import jax.numpy as jnp
from jax import lax
from jax.experimental import pallas as pl
from jax.experimental.pallas import tpu as pltpu
from jax.sharding import PartitionSpec as P

L = 12288
F = 8
S = 8
SIMS = 8
M = 2
Y, X, CORES = 4, 2, 2
CHIPS = Y * X
N = CHIPS * CORES
WIDE = 256
PIECES = ((0, 0, 768), (1, 0, 512), (1, 512, 256))

MESH = pl.DeviceIdType.MESH
F32 = jnp.float32
BF16 = jnp.bfloat16

CHIP_STEPS = ((2, 1), (2, 0), (1, 1), (3, 1), (0, 1), (1, 0), (3, 0))
LINKS = {(0, 0): 0, (0, 1): 1, (1, 0): 1, (3, 0): 1, (2, 0): 2, (1, 1): 2, (3, 1): 2, (2, 1): 3}
STEPS = tuple((dy, dx, dc) for dy, dx in CHIP_STEPS for dc in range(CORES)) + ((0, 0, 1),)


def halves(value):
    high = value.astype(BF16)
    return high, (value - high.astype(F32)).astype(BF16)


def dot(a, b, dims=((1,), (0,))):
    return lax.dot_general(a, b, (dims, ((), ())), preferred_element_type=F32)


def kernel(
    cycles_hbm, legendre_hbm, weight_hbm, filter_hbm, hit_hbm, flux_hbm, order_ref, out_ref,
    own_cycles, own_weight, filters, hits, flux, load_sem,
    injected, injected_t, inj_send, inj_recv, pair_sem, round_sem,
    responses, resp_send, resp_recv,
    blocks, block_send, block_recv, own_sem,
    high, low, harmonics, matched, total, from_core, core_send, core_recv, outgoing, arriving, kept, sum_send, sum_recv,
):
    me = lax.axis_index("blk")
    y, x, core = me // (X * CORES), (me // CORES) % X, me % CORES
    chip = me // CORES
    rows = own_cycles.shape[1]
    half = CHIPS * rows
    degrees = filters.shape[2]

    def chip_at(dy, dx):
        return ((y + dy) % Y) * X + (x + dx) % X

    def at(dy, dx, dc):
        return {"blk": chip_at(dy, dx) * CORES + (core + dc) % CORES}

    barrier = pltpu.get_barrier_semaphore()
    near = [step for step in STEPS if LINKS[step[:2]] <= 1]
    for step in near:
        pl.semaphore_signal(barrier, inc=1, device_id=at(*step), device_id_type=MESH)

    loads = [
        pltpu.make_async_copy(source, target, load_sem.at[i])
        for i, (source, target) in enumerate(
            ((cycles_hbm, own_cycles), (weight_hbm, own_weight), (hit_hbm, hits), (flux_hbm, flux), (filter_hbm, filters))
        )
    ]
    for load in loads:
        load.start()

    own_rows = pl.ds(pl.multiple_of(half + chip * rows, rows), rows)

    def own_copy(q):
        k, first, wide = PIECES[q]
        return pltpu.make_async_copy(
            legendre_hbm.at[k, :, pl.ds(pl.multiple_of(me * degrees + first, 128), wide)],
            blocks.at[k, own_rows, pl.ds(first, wide)],
            own_sem.at[q],
        )

    def block_copy(q, i):
        k, first, wide = PIECES[q]
        dy, dx, dc = STEPS[i]
        there = chip_at(dy, dx) * CORES + (core + dc) % CORES
        return pltpu.make_async_remote_copy(
            src_ref=legendre_hbm.at[k, :, pl.ds(pl.multiple_of(there * degrees + first, 128), wide)],
            dst_ref=blocks.at[
                k, pl.ds(pl.multiple_of((1 - dc) * half + chip * rows, rows), rows), pl.ds(first, wide)
            ],
            send_sem=block_send.at[q, i],
            recv_sem=block_recv.at[q, i],
            device_id={"blk": there},
            device_id_type=MESH,
        )

    for links in range(1, 4):
        if links == 1:
            pl.semaphore_wait(barrier, len(near))
        else:
            pl.semaphore_wait(round_sem.at[links - 2], 3)
        if links < 3:
            for dy, dx in ((0, 1), (1, 0), (3, 0)):
                pl.semaphore_signal(round_sem.at[links - 1], inc=1, device_id=at(dy, dx, 0), device_id_type=MESH)
        for i, step in enumerate(STEPS):
            if LINKS[step[:2]] == links or (links == 1 and step == (0, 0, 1)):
                block_copy(0, i).start()
    own_copy(0).start()

    for load in loads[:4]:
        load.wait()
    row = lax.broadcasted_iota(jnp.int32, (rows, rows), 0)
    lane = lax.broadcasted_iota(jnp.int32, (rows, rows), 1)
    weight = jnp.sum(jnp.where(row == lane, own_weight[...], 0.0), axis=1, keepdims=True)
    for k in range(M):
        clusters = hits.shape[1]
        cycle = me * rows + lax.broadcasted_iota(jnp.int32, (rows, clusters), 0)
        hit = (cycle == hits[k : k + 1, :]).astype(F32)
        added = lax.dot_general(
            hit, flux[k], (((1,), (0,)), ((), ())), precision=lax.Precision.HIGHEST, preferred_element_type=F32
        )
        injected[k, own_rows, :] = weight * (own_cycles[k] + added)

    loads[4].wait()
    degree = me * degrees + lax.broadcasted_iota(jnp.int32, (1, degrees), 1)
    squares = jnp.sum(filters[...] * filters[...], axis=1)
    scale_of = (lax.broadcasted_iota(jnp.int32, (S, 128), 1) // SIMS) % S == lax.broadcasted_iota(jnp.int32, (S, 128), 0)
    for k in range(M):
        factor = jnp.where(degree >= order_ref[k], 2.0 * degree.astype(F32) + 1.0, 0.0)
        response = jnp.sum(squares * factor, axis=1, keepdims=True)
        responses[CHIPS + chip, k : k + 1, :] = jnp.sum(jnp.where(scale_of, response, 0.0), axis=0, keepdims=True)

    inj_copies = [
        pltpu.make_async_remote_copy(
            src_ref=injected.at[:, own_rows, :],
            dst_ref=injected.at[:, own_rows, :],
            send_sem=inj_send.at[i],
            recv_sem=inj_recv.at[i],
            device_id=at(dy, dx, 0),
            device_id_type=MESH,
        )
        for i, (dy, dx) in enumerate(CHIP_STEPS)
    ]
    for copy in inj_copies:
        copy.start()
    resp_copies = [
        pltpu.make_async_remote_copy(
            src_ref=responses.at[CHIPS + chip],
            dst_ref=responses.at[CHIPS + chip],
            send_sem=resp_send.at[i],
            recv_sem=resp_recv.at[i],
            device_id=at(dy, dx, 0),
            device_id_type=MESH,
        )
        for i, (dy, dx) in enumerate(CHIP_STEPS)
    ]
    for copy in resp_copies:
        copy.start()
    for q in range(1, len(PIECES)):
        for i in range(N - 1):
            block_copy(q, i).start()
        own_copy(q).start()

    total[...] = jnp.zeros_like(total)
    for copy in inj_copies:
        copy.wait_recv()
    for copy in resp_copies:
        copy.wait_recv()
    pairs = [
        pltpu.make_async_remote_copy(
            src_ref=source,
            dst_ref=target,
            send_sem=pair_sem.at[i, 0],
            recv_sem=pair_sem.at[i, 1],
            device_id=at(0, 0, 1),
            device_id_type=MESH,
        )
        for i, (source, target) in enumerate(
            (
                (injected.at[:, pl.ds(half, half), :], injected.at[:, pl.ds(0, half), :]),
                (responses.at[pl.ds(CHIPS, CHIPS)], responses.at[pl.ds(0, CHIPS)]),
            )
        )
    ]
    for copy in pairs:
        copy.start()
    for copy in pairs:
        copy.wait_recv()
    for k in range(M):
        turned = jnp.transpose(injected[k])
        turned_high, turned_low = halves(turned)
        injected_t[k, 0:128, :] = turned_high
        injected_t[k, 128:256, :] = turned_low

    def core_copy(k):
        return pltpu.make_async_remote_copy(
            src_ref=total.at[k, pl.ds(0, half), :],
            dst_ref=from_core.at[k],
            send_sem=core_send.at[k],
            recv_sem=core_recv.at[k],
            device_id=at(0, 0, 1),
            device_id_type=MESH,
        )

    def sum_copy(k, i):
        dy, dx = CHIP_STEPS[i]
        return pltpu.make_async_remote_copy(
            src_ref=outgoing.at[k, i],
            dst_ref=arriving.at[k, i],
            send_sem=sum_send.at[k, i],
            recv_sem=sum_recv.at[k, i],
            device_id=at(dy, dx, 0),
            device_id_type=MESH,
        )

    def send_sums(k):
        core_copy(k).wait_recv()
        for i, (dy, dx) in enumerate(CHIP_STEPS):
            there = chip_at(dy, dx) * rows
            outgoing[k, i] = (
                total[k, pl.ds(pl.multiple_of(half + there, rows), rows), :]
                + from_core[k, pl.ds(pl.multiple_of(there, rows), rows), :]
            )
        kept[k] = total[k, own_rows, :] + from_core[k, pl.ds(pl.multiple_of(chip * rows, rows), rows), :]
        for i in range(CHIPS - 1):
            sum_copy(k, i).start()

    def take_sums(k):
        value = kept[k]
        for i in range(CHIPS - 1):
            sum_copy(k, i).wait_recv()
            value = value + arriving[k, i]
        out_ref[k] = value * scale[k : k + 1, :]

    parts = degrees // WIDE

    def part_of(n, carry):
        k = n // parts
        for q, (slot, first, _) in enumerate(PIECES):

            @pl.when(n == slot * parts + first // WIDE)
            def _():
                own_copy(q).wait()
                for i in range(N - 1):
                    block_copy(q, i).wait_recv()

        start = pl.multiple_of((n % parts) * WIDE, WIDE)
        degree = me * degrees + start + lax.broadcasted_iota(jnp.int32, (1, WIDE), 1)
        block_high, block_low = halves(blocks[k, :, pl.ds(start, WIDE)])
        high[...] = block_high
        low[...] = block_low
        first = dot(injected_t[k], high[...])
        second = dot(injected_t[k, 0:128], low[...])
        value = first[0:128] + first[128:256] + second
        harmonics[...] = jnp.where(degree >= order_ref[k], value, 0.0)
        for t in range(WIDE // 128):
            lanes = pl.ds(t * 128, 128)
            for s in range(S):
                sums = [None, None]
                for f in range(F):
                    row = filters[s, f : f + 1, pl.ds(start + t * 128, 128)]
                    for p in range(2):
                        term = row * harmonics[pl.ds((p * F + f) * SIMS, SIMS), lanes]
                        sums[p] = term if f == 0 else sums[p] + term
                for p in range(2):
                    out_high, out_low = halves(sums[p])
                    matched[pl.ds((p * S + s) * SIMS, SIMS), lanes] = out_high
                    matched[pl.ds(128 + (p * S + s) * SIMS, SIMS), lanes] = out_low
        for part in range(2):
            span = pl.ds(part * half, half)
            both = dot(high[span, :], matched[...], ((1,), (1,)))
            third = dot(low[span, :], matched[0:128], ((1,), (1,)))
            total[k, span, :] += both[:, 0:128] + both[:, 128:256] + third
            if part == 0:

                @pl.when(n % parts == parts - 1)
                def _():
                    core_copy(k).start()

        @pl.when(n == parts)
        def _():
            send_sums(0)

        return carry

    lax.fori_loop(0, M * parts, part_of, 0)

    send_sums(1)
    scale = L / jnp.sqrt(jnp.sum(responses[...], axis=0))
    take_sums(0)
    take_sums(1)

    for copy in inj_copies + resp_copies + pairs:
        copy.wait_send()
    for k in range(M):
        core_copy(k).wait_send()
        for i in range(CHIPS - 1):
            sum_copy(k, i).wait_send()
    for q in range(len(PIECES)):
        for i in range(N - 1):
            block_copy(q, i).wait_send()


def body(cycles, legendre, weight, filters, hits, flux, order):
    orders, rows, width = cycles.shape
    degrees = filters.shape[0]
    clusters = hits.shape[1]
    everyone = N * rows
    dma = pltpu.SemaphoreType.DMA
    anywhere = pl.BlockSpec(memory_space=pl.ANY)
    return pl.pallas_call(
        kernel,
        out_shape=jax.ShapeDtypeStruct(cycles.shape, F32),
        in_specs=[anywhere] * 6 + [pl.BlockSpec(memory_space=pltpu.SMEM)],
        out_specs=pl.BlockSpec(memory_space=pltpu.VMEM),
        scratch_shapes=[
            pltpu.VMEM((orders, rows, width), F32),
            pltpu.VMEM((1, rows), F32),
            pltpu.VMEM((S, F, degrees), F32),
            pltpu.VMEM((orders, clusters), jnp.int32),
            pltpu.VMEM((orders, clusters, width), F32),
            dma((5,)),
            pltpu.VMEM((orders, everyone, width), F32),
            pltpu.VMEM((orders, 2 * width, everyone), BF16),
            dma((CHIPS - 1,)),
            dma((CHIPS - 1,)),
            dma((2, 2)),
            pltpu.SemaphoreType.REGULAR((2,)),
            pltpu.VMEM((N, orders, width), F32),
            dma((CHIPS - 1,)),
            dma((CHIPS - 1,)),
            pltpu.VMEM((orders, everyone, degrees), F32),
            dma((len(PIECES), N - 1)),
            dma((len(PIECES), N - 1)),
            dma((len(PIECES),)),
            pltpu.VMEM((everyone, WIDE), BF16),
            pltpu.VMEM((everyone, WIDE), BF16),
            pltpu.VMEM((width, WIDE), F32),
            pltpu.VMEM((2 * width, WIDE), BF16),
            pltpu.VMEM((orders, everyone, width), F32),
            pltpu.VMEM((orders, everyone // 2, width), F32),
            dma((orders,)),
            dma((orders,)),
            pltpu.VMEM((orders, CHIPS - 1, rows, width), F32),
            pltpu.VMEM((orders, CHIPS - 1, rows, width), F32),
            pltpu.VMEM((orders, rows, width), F32),
            dma((orders, CHIPS - 1)),
            dma((orders, CHIPS - 1)),
        ],
        compiler_params=pltpu.CompilerParams(
            collective_id=0, has_side_effects=True, vmem_limit_bytes=60 * 1024 * 1024
        ),
    )(cycles, legendre, weight.reshape(1, rows), jnp.transpose(filters, (1, 2, 0)), hits, flux, order)


def solution(mesh):
    return jax.shard_map(
        body,
        mesh=mesh,
        in_specs=(
            P("order", "blk", None),
            P("order", "blk", None),
            P("blk"),
            P("blk", None, None),
            P("order", None),
            P("order", None, None),
            P("order"),
        ),
        out_specs=P("order", "blk", None),
        check_vma=False,
    )
```

time: 56.3 us -> 54.2 us (0.963)
  Pallas kernels: 54.7 us -> 52.4 us
    pallas_call x1, Pallas kernels: 54.7 us -> 52.4 us  [body(): pl.pallas_call(kernel, out_shape=jax.ShapeDtypeStruct(cycles.shape, F32),...]
where the time goes in v2:
time: 54.2 us; the launch traced here: 53.8 us
  Pallas kernels  52.4 us (97%)
  local copies, waits for them, and re-layouts  1.38 us (3%)
    pallas_call x1, Pallas kernels, body(): pl.pallas_call(kernel, out_shape=jax.ShapeDtypeStruct(cycles.shape, F32),...  52.4 us
    unnamed x1, local copies, waits for them, and re-layouts  1.38 us

profile of v2, /device:TPU:1, one launch (start us, length us, event | category | flops | bytes accessed | tf_op | source)
XLA Modules:
  0.0 53.8 jit_solution(4834152708971651078)
XLA Ops:
  0.0 52.4 %shard_map.73 = f32[2,32,128]{2,1,0:T(8,128)} custom-call(f32[2,32,128]{2,1,0:T(8,128)} %cycles_hbm.1, f32[2,32,12288]{2,1,0:T(8,128)} %legendre_hbm.1, f32[1,32]{1,0:T(1,128)} %bitcast.3, f32[8,8,768]{2,1,0:T(8,128)} %bitcast.2, s32[2,64]{1,0:T(2,128)} %hit_hbm.1, f32[2,64,128]{2,1,0:T(8,128)} %flux_hbm.1, s32[2]{0:T(128)} %order_ref.1), custom_call_target="tpu_custom_call" | custom-call | tf_op jit(solution)/shard_map/pallas_call | solution.py:313
  52.4 1.4 %copy.9 = f32[2,32,128]{2,1,0:T(8,128)} copy(f32[2,32,128]{2,1,0:T(8,128)} %shard_map.73) | data formatting | bytes 65536

commit v3 on v2

--- a/solution.py
+++ b/solution.py
@@ -23,7 +23,6 @@
 BF16 = jnp.bfloat16
 
 CHIP_STEPS = ((2, 1), (2, 0), (1, 1), (3, 1), (0, 1), (1, 0), (3, 0))
-LINKS = {(0, 0): 0, (0, 1): 1, (1, 0): 1, (3, 0): 1, (2, 0): 2, (1, 1): 2, (3, 1): 2, (2, 1): 3}
 STEPS = tuple((dy, dx, dc) for dy, dx in CHIP_STEPS for dc in range(CORES)) + ((0, 0, 1),)
 
 
@@ -37,9 +36,9 @@
 
 
 def kernel(
-    cycles_hbm, legendre_hbm, weight_hbm, filter_hbm, hit_hbm, flux_hbm, order_ref, out_ref,
-    own_cycles, own_weight, filters, hits, flux, load_sem,
-    injected, injected_t, inj_send, inj_recv, pair_sem, round_sem,
+    cycles_hbm, legendre_hbm, weight_hbm, filter_hbm, hit_hbm, flux_hbm, order_hbm, out_ref,
+    order_ref, own_cycles, own_weight, filters, hits, flux, load_sem,
+    injected, injected_t, inj_send, inj_recv, pair_sem,
     responses, resp_send, resp_recv,
     blocks, block_send, block_recv, own_sem,
     high, low, harmonics, matched, total, from_core, core_send, core_recv, outgoing, arriving, kept, sum_send, sum_recv,
@@ -58,14 +57,13 @@
         return {"blk": chip_at(dy, dx) * CORES + (core + dc) % CORES}
 
     barrier = pltpu.get_barrier_semaphore()
-    near = [step for step in STEPS if LINKS[step[:2]] <= 1]
-    for step in near:
+    for step in STEPS:
         pl.semaphore_signal(barrier, inc=1, device_id=at(*step), device_id_type=MESH)
 
     loads = [
         pltpu.make_async_copy(source, target, load_sem.at[i])
         for i, (source, target) in enumerate(
-            ((cycles_hbm, own_cycles), (weight_hbm, own_weight), (hit_hbm, hits), (flux_hbm, flux), (filter_hbm, filters))
+            ((cycles_hbm, own_cycles), (weight_hbm, own_weight), (hit_hbm, hits), (flux_hbm, flux), (filter_hbm, filters), (order_hbm, order_ref))
         )
     ]
     for load in loads:
@@ -96,17 +94,9 @@
             device_id_type=MESH,
         )
 
-    for links in range(1, 4):
-        if links == 1:
-            pl.semaphore_wait(barrier, len(near))
-        else:
-            pl.semaphore_wait(round_sem.at[links - 2], 3)
-        if links < 3:
-            for dy, dx in ((0, 1), (1, 0), (3, 0)):
-                pl.semaphore_signal(round_sem.at[links - 1], inc=1, device_id=at(dy, dx, 0), device_id_type=MESH)
-        for i, step in enumerate(STEPS):
-            if LINKS[step[:2]] == links or (links == 1 and step == (0, 0, 1)):
-                block_copy(0, i).start()
+    pl.semaphore_wait(barrier, N - 1)
+    for i in range(N - 1):
+        block_copy(0, i).start()
     own_copy(0).start()
 
     for load in loads[:4]:
@@ -124,6 +114,7 @@
         injected[k, own_rows, :] = weight * (own_cycles[k] + added)
 
     loads[4].wait()
+    loads[5].wait()
     degree = me * degrees + lax.broadcasted_iota(jnp.int32, (1, degrees), 1)
     squares = jnp.sum(filters[...] * filters[...], axis=1)
     scale_of = (lax.broadcasted_iota(jnp.int32, (S, 128), 1) // SIMS) % S == lax.broadcasted_iota(jnp.int32, (S, 128), 0)
@@ -312,22 +303,22 @@
     anywhere = pl.BlockSpec(memory_space=pl.ANY)
     return pl.pallas_call(
         kernel,
-        out_shape=jax.ShapeDtypeStruct(cycles.shape, F32),
-        in_specs=[anywhere] * 6 + [pl.BlockSpec(memory_space=pltpu.SMEM)],
+        out_shape=pltpu.VMEM(cycles.shape, F32),
+        in_specs=[anywhere] * 7,
         out_specs=pl.BlockSpec(memory_space=pltpu.VMEM),
         scratch_shapes=[
+            pltpu.SMEM((orders,), jnp.int32),
             pltpu.VMEM((orders, rows, width), F32),
             pltpu.VMEM((1, rows), F32),
             pltpu.VMEM((S, F, degrees), F32),
             pltpu.VMEM((orders, clusters), jnp.int32),
             pltpu.VMEM((orders, clusters, width), F32),
-            dma((5,)),
+            dma((6,)),
             pltpu.VMEM((orders, everyone, width), F32),
             pltpu.VMEM((orders, 2 * width, everyone), BF16),
             dma((CHIPS - 1,)),
             dma((CHIPS - 1,)),
             dma((2, 2)),
-            pltpu.SemaphoreType.REGULAR((2,)),
             pltpu.VMEM((N, orders, width), F32),
             dma((CHIPS - 1,)),
             dma((CHIPS - 1,)),

time: 54.2 us -> 51.8 us (0.956)
  Pallas kernels: 52.4 us -> 51.1 us
  local copies, waits for them, and re-layouts: 1.38 us -> 0.62 us
    pallas_call x1, Pallas kernels: 52.4 us -> 51.1 us  [body(): pl.pallas_call(kernel, out_shape=pltpu.VMEM(cycles.shape, F32), in_specs=...]
    unnamed x1, local copies, waits for them, and re-layouts: 1.38 us -> 0.62 us
where the time goes in v3:
time: 51.8 us; the launch traced here: 51.7 us
  Pallas kernels  51.1 us (99%)
  local copies, waits for them, and re-layouts  0.62 us (1%)
    pallas_call x1, Pallas kernels, body(): pl.pallas_call(kernel, out_shape=pltpu.VMEM(cycles.shape, F32), in_specs=...  51.1 us

profile of v3, /device:TPU:1, one launch (start us, length us, event | category | flops | bytes accessed | tf_op | source)
XLA Modules:
  0.0 51.7 jit_solution(9621915556996838867)
XLA Ops:
  0.0 51.1 %shard_map.73 = f32[2,32,128]{2,1,0:T(8,128)S(1)} custom-call(f32[2,32,128]{2,1,0:T(8,128)} %cycles_hbm.1, f32[2,32,12288]{2,1,0:T(8,128)} %legendre_hbm.1, f32[1,32]{1,0:T(1,128)} %bitcast.3, f32[8,8,768]{2,1,0:T(8,128)} %bitcast.2, s32[2,64]{1,0:T(2,128)} %hit_hbm.1, f32[2,64,128]{2,1,0:T(8,128)} %flux_hbm.1, s32[2]{0:T(128)} %order_hbm.1), custom_call_target="tpu_custom_call" | custom-call | tf_op jit(solution)/shard_map/pallas_call | solution.py:304
  51.1 0.6 %copy.9 = f32[2,32,128]{2,1,0:T(8,128)} copy(f32[2,32,128]{2,1,0:T(8,128)S(1)} %shard_map.73) | data formatting | bytes 65536

commit v4 on v3

--- a/solution.py
+++ b/solution.py
@@ -23,12 +23,17 @@
 BF16 = jnp.bfloat16
 
 CHIP_STEPS = ((2, 1), (2, 0), (1, 1), (3, 1), (0, 1), (1, 0), (3, 0))
+RELAYS = ((0, 1), (2, 0), (1, 0), (3, 0))
 STEPS = tuple((dy, dx, dc) for dy, dx in CHIP_STEPS for dc in range(CORES)) + ((0, 0, 1),)
 
 
 def halves(value):
     high = value.astype(BF16)
     return high, (value - high.astype(F32)).astype(BF16)
+
+
+def take(ref, sem):
+    pltpu.make_async_copy(ref, ref, sem).wait()
 
 
 def dot(a, b, dims=((1,), (0,))):
@@ -40,7 +45,7 @@
     order_ref, own_cycles, own_weight, filters, hits, flux, load_sem,
     injected, injected_t, inj_send, inj_recv, pair_sem,
     responses, resp_send, resp_recv,
-    blocks, block_send, block_recv, own_sem,
+    blocks, block_send, block_recv,
     high, low, harmonics, matched, total, from_core, core_send, core_recv, outgoing, arriving, kept, sum_send, sum_recv,
 ):
     me = lax.axis_index("blk")
@@ -76,7 +81,7 @@
         return pltpu.make_async_copy(
             legendre_hbm.at[k, :, pl.ds(pl.multiple_of(me * degrees + first, 128), wide)],
             blocks.at[k, own_rows, pl.ds(first, wide)],
-            own_sem.at[q],
+            block_recv.at[q],
         )
 
     def block_copy(q, i):
@@ -88,16 +93,11 @@
             dst_ref=blocks.at[
                 k, pl.ds(pl.multiple_of((1 - dc) * half + chip * rows, rows), rows), pl.ds(first, wide)
             ],
-            send_sem=block_send.at[q, i],
-            recv_sem=block_recv.at[q, i],
+            send_sem=block_send.at[0],
+            recv_sem=block_recv.at[q],
             device_id={"blk": there},
             device_id_type=MESH,
         )
-
-    pl.semaphore_wait(barrier, N - 1)
-    for i in range(N - 1):
-        block_copy(0, i).start()
-    own_copy(0).start()
 
     for load in loads[:4]:
         load.wait()
@@ -113,6 +113,27 @@
         )
         injected[k, own_rows, :] = weight * (own_cycles[k] + added)
 
+    across = chip_at(0, 1)
+
+    def inj_copy(i):
+        source, (dy, dx) = ((chip, RELAYS[i]) if i < 4 else (across, RELAYS[i - 3]))
+        place = injected.at[:, pl.ds(pl.multiple_of(half + source * rows, rows), rows), :]
+        return pltpu.make_async_remote_copy(
+            src_ref=place,
+            dst_ref=place,
+            send_sem=inj_send.at[0],
+            recv_sem=inj_recv.at[0 if i == 0 else 1],
+            device_id=at(dy, dx, 0),
+            device_id_type=MESH,
+        )
+
+    pl.semaphore_wait(barrier, N - 1)
+    for i in range(4):
+        inj_copy(i).start()
+    for i in range(N - 1):
+        block_copy(0, i).start()
+    own_copy(0).start()
+
     loads[4].wait()
     loads[5].wait()
     degree = me * degrees + lax.broadcasted_iota(jnp.int32, (1, degrees), 1)
@@ -123,42 +144,30 @@
         response = jnp.sum(squares * factor, axis=1, keepdims=True)
         responses[CHIPS + chip, k : k + 1, :] = jnp.sum(jnp.where(scale_of, response, 0.0), axis=0, keepdims=True)
 
-    inj_copies = [
-        pltpu.make_async_remote_copy(
-            src_ref=injected.at[:, own_rows, :],
-            dst_ref=injected.at[:, own_rows, :],
-            send_sem=inj_send.at[i],
-            recv_sem=inj_recv.at[i],
-            device_id=at(dy, dx, 0),
-            device_id_type=MESH,
-        )
-        for i, (dy, dx) in enumerate(CHIP_STEPS)
-    ]
-    for copy in inj_copies:
-        copy.start()
     resp_copies = [
         pltpu.make_async_remote_copy(
             src_ref=responses.at[CHIPS + chip],
             dst_ref=responses.at[CHIPS + chip],
-            send_sem=resp_send.at[i],
-            recv_sem=resp_recv.at[i],
+            send_sem=resp_send.at[0],
+            recv_sem=resp_recv.at[0],
             device_id=at(dy, dx, 0),
             device_id_type=MESH,
         )
-        for i, (dy, dx) in enumerate(CHIP_STEPS)
+        for dy, dx in CHIP_STEPS
     ]
     for copy in resp_copies:
         copy.start()
+    inj_copy(0).wait_recv()
+    for i in range(4, CHIPS - 1):
+        inj_copy(i).start()
     for q in range(1, len(PIECES)):
         for i in range(N - 1):
             block_copy(q, i).start()
         own_copy(q).start()
 
     total[...] = jnp.zeros_like(total)
-    for copy in inj_copies:
-        copy.wait_recv()
-    for copy in resp_copies:
-        copy.wait_recv()
+    take(injected.at[:, pl.ds(0, (CHIPS - 2) * rows), :], inj_recv.at[1])
+    take(responses.at[pl.ds(0, CHIPS - 1)], resp_recv.at[0])
     pairs = [
         pltpu.make_async_remote_copy(
             src_ref=source,
@@ -200,8 +209,8 @@
         return pltpu.make_async_remote_copy(
             src_ref=outgoing.at[k, i],
             dst_ref=arriving.at[k, i],
-            send_sem=sum_send.at[k, i],
-            recv_sem=sum_recv.at[k, i],
+            send_sem=sum_send.at[k],
+            recv_sem=sum_recv.at[k],
             device_id=at(dy, dx, 0),
             device_id_type=MESH,
         )
@@ -220,8 +229,8 @@
 
     def take_sums(k):
         value = kept[k]
+        take(arriving.at[k], sum_recv.at[k])
         for i in range(CHIPS - 1):
-            sum_copy(k, i).wait_recv()
             value = value + arriving[k, i]
         out_ref[k] = value * scale[k : k + 1, :]
 
@@ -229,13 +238,11 @@
 
     def part_of(n, carry):
         k = n // parts
-        for q, (slot, first, _) in enumerate(PIECES):
+        for q, (slot, first, wide) in enumerate(PIECES):
 
             @pl.when(n == slot * parts + first // WIDE)
             def _():
-                own_copy(q).wait()
-                for i in range(N - 1):
-                    block_copy(q, i).wait_recv()
+                take(blocks.at[slot, :, pl.ds(first, wide)], block_recv.at[q])
 
         start = pl.multiple_of((n % parts) * WIDE, WIDE)
         degree = me * degrees + start + lax.broadcasted_iota(jnp.int32, (1, WIDE), 1)
@@ -283,15 +290,14 @@
     take_sums(0)
     take_sums(1)
 
-    for copy in inj_copies + resp_copies + pairs:
+    take(injected.at[:, pl.ds(0, (CHIPS - 1) * rows), :], inj_send.at[0])
+    take(responses.at[pl.ds(0, CHIPS - 1)], resp_send.at[0])
+    for copy in pairs:
         copy.wait_send()
     for k in range(M):
         core_copy(k).wait_send()
-        for i in range(CHIPS - 1):
-            sum_copy(k, i).wait_send()
-    for q in range(len(PIECES)):
-        for i in range(N - 1):
-            block_copy(q, i).wait_send()
+        take(outgoing.at[k], sum_send.at[k])
+    take(blocks.at[:, pl.ds(0, (N - 1) * rows), :], block_send.at[0])
 
 
 def body(cycles, legendre, weight, filters, hits, flux, order):
@@ -316,15 +322,14 @@
             dma((6,)),
             pltpu.VMEM((orders, everyone, width), F32),
             pltpu.VMEM((orders, 2 * width, everyone), BF16),
-            dma((CHIPS - 1,)),
-            dma((CHIPS - 1,)),
+            dma((1,)),
+            dma((2,)),
             dma((2, 2)),
             pltpu.VMEM((N, orders, width), F32),
-            dma((CHIPS - 1,)),
-            dma((CHIPS - 1,)),
+            dma((1,)),
+            dma((1,)),
             pltpu.VMEM((orders, everyone, degrees), F32),
-            dma((len(PIECES), N - 1)),
-            dma((len(PIECES), N - 1)),
+            dma((1,)),
             dma((len(PIECES),)),
             pltpu.VMEM((everyone, WIDE), BF16),
             pltpu.VMEM((everyone, WIDE), BF16),
@@ -337,8 +342,8 @@
             pltpu.VMEM((orders, CHIPS - 1, rows, width), F32),
             pltpu.VMEM((orders, CHIPS - 1, rows, width), F32),
             pltpu.VMEM((orders, rows, width), F32),
-            dma((orders, CHIPS - 1)),
-            dma((orders, CHIPS - 1)),
+            dma((orders,)),
+            dma((orders,)),
         ],
         compiler_params=pltpu.CompilerParams(
             collective_id=0, has_side_effects=True, vmem_limit_bytes=60 * 1024 * 1024

time: 51.8 us -> 50.1 us (0.967)
  Pallas kernels: 51.1 us -> 49.3 us
    pallas_call x1, Pallas kernels: 51.1 us -> 49.3 us  [body(): pl.pallas_call(kernel, out_shape=pltpu.VMEM(cycles.shape, F32), in_specs=...]
where the time goes in v4:
time: 50.1 us; the launch traced here: 50 us
  Pallas kernels  49.3 us (98%)
  local copies, waits for them, and re-layouts  0.62 us (1%)
    pallas_call x1, Pallas kernels, body(): pl.pallas_call(kernel, out_shape=pltpu.VMEM(cycles.shape, F32), in_specs=...  49.3 us

profile of v4, /device:TPU:1, one launch (start us, length us, event | category | flops | bytes accessed | tf_op | source)
XLA Modules:
  0.0 50.0 jit_solution(11985727149434733638)
XLA Ops:
  0.0 49.3 %shard_map.73 = f32[2,32,128]{2,1,0:T(8,128)S(1)} custom-call(f32[2,32,128]{2,1,0:T(8,128)} %cycles_hbm.1, f32[2,32,12288]{2,1,0:T(8,128)} %legendre_hbm.1, f32[1,32]{1,0:T(1,128)} %bitcast.3, f32[8,8,768]{2,1,0:T(8,128)} %bitcast.2, s32[2,64]{1,0:T(2,128)} %hit_hbm.1, f32[2,64,128]{2,1,0:T(8,128)} %flux_hbm.1, s32[2]{0:T(128)} %order_hbm.1), custom_call_target="tpu_custom_call" | custom-call | tf_op jit(solution)/shard_map/pallas_call | solution.py:310
  49.4 0.6 %copy.9 = f32[2,32,128]{2,1,0:T(8,128)} copy(f32[2,32,128]{2,1,0:T(8,128)S(1)} %shard_map.73) | data formatting | bytes 65536

commit v5 on v4

--- a/solution.py
+++ b/solution.py
@@ -113,23 +113,24 @@
         )
         injected[k, own_rows, :] = weight * (own_cycles[k] + added)
 
-    across = chip_at(0, 1)
-
-    def inj_copy(i):
-        source, (dy, dx) = ((chip, RELAYS[i]) if i < 4 else (across, RELAYS[i - 3]))
-        place = injected.at[:, pl.ds(pl.multiple_of(half + source * rows, rows), rows), :]
+    def inj_copy(ks, source, step, sem):
+        place = injected.at[ks, pl.ds(pl.multiple_of(half + source * rows, rows), rows), :]
         return pltpu.make_async_remote_copy(
             src_ref=place,
             dst_ref=place,
-            send_sem=inj_send.at[0],
-            recv_sem=inj_recv.at[0 if i == 0 else 1],
-            device_id=at(dy, dx, 0),
-            device_id_type=MESH,
-        )
+            send_sem=inj_send.at[sem],
+            recv_sem=inj_recv.at[sem],
+            device_id=at(*step, 0),
+            device_id_type=MESH,
+        )
+
+    inj_direct = [inj_copy(pl.ds(0, M), chip, step, 0) for step in RELAYS]
+    inj_relayed = [inj_copy(0, chip_at(0, 1), step, 1) for step in RELAYS[1:]]
+    inj_relayed += [inj_copy(1, chip_at(*step), RELAYS[0], 1) for step in RELAYS[1:]]
 
     pl.semaphore_wait(barrier, N - 1)
-    for i in range(4):
-        inj_copy(i).start()
+    for copy in inj_direct:
+        copy.start()
     for i in range(N - 1):
         block_copy(0, i).start()
     own_copy(0).start()
@@ -157,16 +158,16 @@
     ]
     for copy in resp_copies:
         copy.start()
-    inj_copy(0).wait_recv()
-    for i in range(4, CHIPS - 1):
-        inj_copy(i).start()
+    take(injected.at[:, pl.ds(0, 4 * rows), :], inj_recv.at[0])
+    for copy in inj_relayed:
+        copy.start()
     for q in range(1, len(PIECES)):
         for i in range(N - 1):
             block_copy(q, i).start()
         own_copy(q).start()
 
     total[...] = jnp.zeros_like(total)
-    take(injected.at[:, pl.ds(0, (CHIPS - 2) * rows), :], inj_recv.at[1])
+    take(injected.at[:, pl.ds(0, 3 * rows), :], inj_recv.at[1])
     take(responses.at[pl.ds(0, CHIPS - 1)], resp_recv.at[0])
     pairs = [
         pltpu.make_async_remote_copy(
@@ -249,9 +250,13 @@
         block_high, block_low = halves(blocks[k, :, pl.ds(start, WIDE)])
         high[...] = block_high
         low[...] = block_low
-        first = dot(injected_t[k], high[...])
-        second = dot(injected_t[k, 0:128], low[...])
-        value = first[0:128] + first[128:256] + second
+        value = None
+        for h in range(2):
+            span = pl.ds(h * half, half)
+            first = dot(injected_t[k, :, span], high[span, :])
+            second = dot(injected_t[k, 0:128, span], low[span, :])
+            term = first[0:128] + first[128:256] + second
+            value = term if h == 0 else value + term
         harmonics[...] = jnp.where(degree >= order_ref[k], value, 0.0)
         for t in range(WIDE // 128):
             lanes = pl.ds(t * 128, 128)
@@ -290,7 +295,8 @@
     take_sums(0)
     take_sums(1)
 
-    take(injected.at[:, pl.ds(0, (CHIPS - 1) * rows), :], inj_send.at[0])
+    take(injected.at[:, pl.ds(0, 4 * rows), :], inj_send.at[0])
+    take(injected.at[:, pl.ds(0, 3 * rows), :], inj_send.at[1])
     take(responses.at[pl.ds(0, CHIPS - 1)], resp_send.at[0])
     for copy in pairs:
         copy.wait_send()
@@ -322,7 +328,7 @@
             dma((6,)),
             pltpu.VMEM((orders, everyone, width), F32),
             pltpu.VMEM((orders, 2 * width, everyone), BF16),
-            dma((1,)),
+            dma((2,)),
             dma((2,)),
             dma((2, 2)),
             pltpu.VMEM((N, orders, width), F32),

time: 50.1 us -> 49.6 us (0.990)
  no operation moved by 1% of the time
where the time goes in v5:
time: 49.6 us; the launch traced here: 49.5 us
  Pallas kernels  48.9 us (99%)
  local copies, waits for them, and re-layouts  0.62 us (1%)
    pallas_call x1, Pallas kernels, body(): pl.pallas_call(kernel, out_shape=pltpu.VMEM(cycles.shape, F32), in_specs=...  48.9 us

profile of v5, /device:TPU:1, one launch (start us, length us, event | category | flops | bytes accessed | tf_op | source)
XLA Modules:
  0.0 49.5 jit_solution(11811998149336909347)
XLA Ops:
  0.0 48.9 %shard_map.73 = f32[2,32,128]{2,1,0:T(8,128)S(1)} custom-call(f32[2,32,128]{2,1,0:T(8,128)} %cycles_hbm.1, f32[2,32,12288]{2,1,0:T(8,128)} %legendre_hbm.1, f32[1,32]{1,0:T(1,128)} %bitcast.3, f32[8,8,768]{2,1,0:T(8,128)} %bitcast.2, s32[2,64]{1,0:T(2,128)} %hit_hbm.1, f32[2,64,128]{2,1,0:T(8,128)} %flux_hbm.1, s32[2]{0:T(128)} %order_hbm.1), custom_call_target="tpu_custom_call" | custom-call | tf_op jit(solution)/shard_map/pallas_call | solution.py:316
  48.9 0.6 %copy.9 = f32[2,32,128]{2,1,0:T(8,128)} copy(f32[2,32,128]{2,1,0:T(8,128)S(1)} %shard_map.73) | data formatting | bytes 65536

commit v6 on v5

--- a/solution.py
+++ b/solution.py
@@ -16,6 +16,7 @@
 CHIPS = Y * X
 N = CHIPS * CORES
 WIDE = 256
+SPLIT = 2
 PIECES = ((0, 0, 768), (1, 0, 512), (1, 512, 256))
 
 MESH = pl.DeviceIdType.MESH
@@ -23,8 +24,13 @@
 BF16 = jnp.bfloat16
 
 CHIP_STEPS = ((2, 1), (2, 0), (1, 1), (3, 1), (0, 1), (1, 0), (3, 0))
+PLACE = {step: i for i, step in enumerate(CHIP_STEPS + ((0, 0),))}
 RELAYS = ((0, 1), (2, 0), (1, 0), (3, 0))
 STEPS = tuple((dy, dx, dc) for dy, dx in CHIP_STEPS for dc in range(CORES)) + ((0, 0, 1),)
+
+
+def back(dy, dx):
+    return (Y - dy) % Y, dx
 
 
 def halves(value):
@@ -50,7 +56,6 @@
 ):
     me = lax.axis_index("blk")
     y, x, core = me // (X * CORES), (me // CORES) % X, me % CORES
-    chip = me // CORES
     rows = own_cycles.shape[1]
     half = CHIPS * rows
     degrees = filters.shape[2]
@@ -74,7 +79,10 @@
     for load in loads:
         load.start()
 
-    own_rows = pl.ds(pl.multiple_of(half + chip * rows, rows), rows)
+    def rows_of(step, same_core=1):
+        return pl.ds(same_core * half + PLACE[step] * rows, rows)
+
+    own_rows = rows_of((0, 0))
 
     def own_copy(q):
         k, first, wide = PIECES[q]
@@ -91,7 +99,7 @@
         return pltpu.make_async_remote_copy(
             src_ref=legendre_hbm.at[k, :, pl.ds(pl.multiple_of(there * degrees + first, 128), wide)],
             dst_ref=blocks.at[
-                k, pl.ds(pl.multiple_of((1 - dc) * half + chip * rows, rows), rows), pl.ds(first, wide)
+                k, rows_of(back(dy, dx), 1 - dc), pl.ds(first, wide)
             ],
             send_sem=block_send.at[0],
             recv_sem=block_recv.at[q],
@@ -114,19 +122,19 @@
         injected[k, own_rows, :] = weight * (own_cycles[k] + added)
 
     def inj_copy(ks, source, step, sem):
-        place = injected.at[ks, pl.ds(pl.multiple_of(half + source * rows, rows), rows), :]
+        seen = ((source[0] - step[0]) % Y, (source[1] - step[1]) % X)
         return pltpu.make_async_remote_copy(
-            src_ref=place,
-            dst_ref=place,
+            src_ref=injected.at[ks, rows_of(source), :],
+            dst_ref=injected.at[ks, rows_of(seen), :],
             send_sem=inj_send.at[sem],
             recv_sem=inj_recv.at[sem],
             device_id=at(*step, 0),
             device_id_type=MESH,
         )
 
-    inj_direct = [inj_copy(pl.ds(0, M), chip, step, 0) for step in RELAYS]
-    inj_relayed = [inj_copy(0, chip_at(0, 1), step, 1) for step in RELAYS[1:]]
-    inj_relayed += [inj_copy(1, chip_at(*step), RELAYS[0], 1) for step in RELAYS[1:]]
+    inj_direct = [inj_copy(pl.ds(0, M), (0, 0), step, 0) for step in RELAYS]
+    inj_relayed = [inj_copy(0, RELAYS[0], step, 1) for step in RELAYS[1:]]
+    inj_relayed += [inj_copy(1, step, RELAYS[0], 1) for step in RELAYS[1:]]
 
     pl.semaphore_wait(barrier, N - 1)
     for copy in inj_direct:
@@ -143,12 +151,12 @@
     for k in range(M):
         factor = jnp.where(degree >= order_ref[k], 2.0 * degree.astype(F32) + 1.0, 0.0)
         response = jnp.sum(squares * factor, axis=1, keepdims=True)
-        responses[CHIPS + chip, k : k + 1, :] = jnp.sum(jnp.where(scale_of, response, 0.0), axis=0, keepdims=True)
+        responses[N - 1, k : k + 1, :] = jnp.sum(jnp.where(scale_of, response, 0.0), axis=0, keepdims=True)
 
     resp_copies = [
         pltpu.make_async_remote_copy(
-            src_ref=responses.at[CHIPS + chip],
-            dst_ref=responses.at[CHIPS + chip],
+            src_ref=responses.at[N - 1],
+            dst_ref=responses.at[CHIPS + PLACE[back(dy, dx)]],
             send_sem=resp_send.at[0],
             recv_sem=resp_recv.at[0],
             device_id=at(dy, dx, 0),
@@ -195,10 +203,11 @@
         injected_t[k, 0:128, :] = turned_high
         injected_t[k, 128:256, :] = turned_low
 
-    def core_copy(k):
+    def core_copy(k, piece):
+        place = pl.ds(piece * half // SPLIT, half // SPLIT)
         return pltpu.make_async_remote_copy(
-            src_ref=total.at[k, pl.ds(0, half), :],
-            dst_ref=from_core.at[k],
+            src_ref=total.at[k, place, :],
+            dst_ref=from_core.at[k, place, :],
             send_sem=core_send.at[k],
             recv_sem=core_recv.at[k],
             device_id=at(0, 0, 1),
@@ -208,7 +217,7 @@
     def sum_copy(k, i):
         dy, dx = CHIP_STEPS[i]
         return pltpu.make_async_remote_copy(
-            src_ref=outgoing.at[k, i],
+            src_ref=outgoing.at[k, pl.ds(i * rows, rows), :],
             dst_ref=arriving.at[k, i],
             send_sem=sum_send.at[k],
             recv_sem=sum_recv.at[k],
@@ -217,14 +226,10 @@
         )
 
     def send_sums(k):
-        core_copy(k).wait_recv()
-        for i, (dy, dx) in enumerate(CHIP_STEPS):
-            there = chip_at(dy, dx) * rows
-            outgoing[k, i] = (
-                total[k, pl.ds(pl.multiple_of(half + there, rows), rows), :]
-                + from_core[k, pl.ds(pl.multiple_of(there, rows), rows), :]
-            )
-        kept[k] = total[k, own_rows, :] + from_core[k, pl.ds(pl.multiple_of(chip * rows, rows), rows), :]
+        take(from_core.at[k], core_recv.at[k])
+        others = (CHIPS - 1) * rows
+        outgoing[k] = total[k, pl.ds(half, others), :] + from_core[k, pl.ds(0, others), :]
+        kept[k] = total[k, own_rows, :] + from_core[k, pl.ds(others, rows), :]
         for i in range(CHIPS - 1):
             sum_copy(k, i).start()
 
@@ -280,7 +285,8 @@
 
                 @pl.when(n % parts == parts - 1)
                 def _():
-                    core_copy(k).start()
+                    for piece in range(SPLIT):
+                        core_copy(k, piece).start()
 
         @pl.when(n == parts)
         def _():
@@ -301,7 +307,7 @@
     for copy in pairs:
         copy.wait_send()
     for k in range(M):
-        core_copy(k).wait_send()
+        take(from_core.at[k], core_send.at[k])
         take(outgoing.at[k], sum_send.at[k])
     take(blocks.at[:, pl.ds(0, (N - 1) * rows), :], block_send.at[0])
 
@@ -345,7 +351,7 @@
             pltpu.VMEM((orders, everyone // 2, width), F32),
             dma((orders,)),
             dma((orders,)),
-            pltpu.VMEM((orders, CHIPS - 1, rows, width), F32),
+            pltpu.VMEM((orders, (CHIPS - 1) * rows, width), F32),
             pltpu.VMEM((orders, CHIPS - 1, rows, width), F32),
             pltpu.VMEM((orders, rows, width), F32),
             dma((orders,)),

time: 49.6 us -> 49.6 us (level)
  no operation moved by 1% of the time
where the time goes in v6:
time: 49.6 us; the launch traced here: 49.5 us
  Pallas kernels  48.9 us (99%)
  local copies, waits for them, and re-layouts  0.62 us (1%)
    pallas_call x1, Pallas kernels, body(): pl.pallas_call(kernel, out_shape=pltpu.VMEM(cycles.shape, F32), in_specs=...  48.9 us

profile of v6, /device:TPU:1, one launch (start us, length us, event | category | flops | bytes accessed | tf_op | source)
XLA Modules:
  0.0 49.5 jit_solution(6623804295078301017)
XLA Ops:
  0.0 48.9 %shard_map.73 = f32[2,32,128]{2,1,0:T(8,128)S(1)} custom-call(f32[2,32,128]{2,1,0:T(8,128)} %cycles_hbm.1, f32[2,32,12288]{2,1,0:T(8,128)} %legendre_hbm.1, f32[1,32]{1,0:T(1,128)} %bitcast.3, f32[8,8,768]{2,1,0:T(8,128)} %bitcast.2, s32[2,64]{1,0:T(2,128)} %hit_hbm.1, f32[2,64,128]{2,1,0:T(8,128)} %flux_hbm.1, s32[2]{0:T(128)} %order_hbm.1), custom_call_target="tpu_custom_call" | custom-call | tf_op jit(solution)/shard_map/pallas_call | solution.py:322
  48.9 0.6 %copy.9 = f32[2,32,128]{2,1,0:T(8,128)} copy(f32[2,32,128]{2,1,0:T(8,128)S(1)} %shard_map.73) | data formatting | bytes 65536

commit v7 on v6

--- a/solution.py
+++ b/solution.py
@@ -209,7 +209,7 @@
             src_ref=total.at[k, place, :],
             dst_ref=from_core.at[k, place, :],
             send_sem=core_send.at[k],
-            recv_sem=core_recv.at[k],
+            recv_sem=core_recv.at[k, piece],
             device_id=at(0, 0, 1),
             device_id_type=MESH,
         )
@@ -226,12 +226,17 @@
         )
 
     def send_sums(k):
-        take(from_core.at[k], core_recv.at[k])
-        others = (CHIPS - 1) * rows
-        outgoing[k] = total[k, pl.ds(half, others), :] + from_core[k, pl.ds(0, others), :]
-        kept[k] = total[k, own_rows, :] + from_core[k, pl.ds(others, rows), :]
-        for i in range(CHIPS - 1):
-            sum_copy(k, i).start()
+        for piece in range(SPLIT):
+            core_copy(k, piece).wait_recv()
+            chips = range(piece * CHIPS // SPLIT, min((piece + 1) * CHIPS // SPLIT, CHIPS - 1))
+            first, size = chips[0] * rows, len(chips) * rows
+            outgoing[k, pl.ds(first, size), :] = (
+                total[k, pl.ds(half + first, size), :] + from_core[k, pl.ds(first, size), :]
+            )
+            if piece == SPLIT - 1:
+                kept[k] = total[k, own_rows, :] + from_core[k, pl.ds((CHIPS - 1) * rows, rows), :]
+            for i in chips:
+                sum_copy(k, i).start()
 
     def take_sums(k):
         value = kept[k]
@@ -350,7 +355,7 @@
             pltpu.VMEM((orders, everyone, width), F32),
             pltpu.VMEM((orders, everyone // 2, width), F32),
             dma((orders,)),
-            dma((orders,)),
+            dma((orders, SPLIT)),
             pltpu.VMEM((orders, (CHIPS - 1) * rows, width), F32),
             pltpu.VMEM((orders, CHIPS - 1, rows, width), F32),
             pltpu.VMEM((orders, rows, width), F32),

time: 49.6 us -> 49.7 us (level)
  no operation moved by 1% of the time
where the time goes in v7:
time: 49.7 us; the launch traced here: 49.6 us
  Pallas kernels  49 us (99%)
  local copies, waits for them, and re-layouts  0.62 us (1%)
    pallas_call x1, Pallas kernels, body(): pl.pallas_call(kernel, out_shape=pltpu.VMEM(cycles.shape, F32), in_specs=...  49 us

profile of v7, /device:TPU:1, one launch (start us, length us, event | category | flops | bytes accessed | tf_op | source)
XLA Modules:
  0.0 49.6 jit_solution(11062575545474356074)
XLA Ops:
  0.0 49.0 %shard_map.73 = f32[2,32,128]{2,1,0:T(8,128)S(1)} custom-call(f32[2,32,128]{2,1,0:T(8,128)} %cycles_hbm.1, f32[2,32,12288]{2,1,0:T(8,128)} %legendre_hbm.1, f32[1,32]{1,0:T(1,128)} %bitcast.3, f32[8,8,768]{2,1,0:T(8,128)} %bitcast.2, s32[2,64]{1,0:T(2,128)} %hit_hbm.1, f32[2,64,128]{2,1,0:T(8,128)} %flux_hbm.1, s32[2]{0:T(128)} %order_hbm.1), custom_call_target="tpu_custom_call" | custom-call | tf_op jit(solution)/shard_map/pallas_call | solution.py:327
  49.0 0.6 %copy.9 = f32[2,32,128]{2,1,0:T(8,128)} copy(f32[2,32,128]{2,1,0:T(8,128)S(1)} %shard_map.73) | data formatting | bytes 65536

commit v8 on v6

--- a/solution.py
+++ b/solution.py
@@ -66,10 +66,6 @@
     def at(dy, dx, dc):
         return {"blk": chip_at(dy, dx) * CORES + (core + dc) % CORES}
 
-    barrier = pltpu.get_barrier_semaphore()
-    for step in STEPS:
-        pl.semaphore_signal(barrier, inc=1, device_id=at(*step), device_id_type=MESH)
-
     loads = [
         pltpu.make_async_copy(source, target, load_sem.at[i])
         for i, (source, target) in enumerate(
@@ -78,6 +74,10 @@
     ]
     for load in loads:
         load.start()
+
+    barrier = pltpu.get_barrier_semaphore()
+    for step in STEPS:
+        pl.semaphore_signal(barrier, inc=1, device_id=at(*step), device_id_type=MESH)
 
     def rows_of(step, same_core=1):
         return pl.ds(same_core * half + PLACE[step] * rows, rows)

time: 49.6 us -> 49.6 us (level)
  no operation moved by 1% of the time
where the time goes in v8:
time: 49.6 us; the launch traced here: 49.5 us
  Pallas kernels  48.9 us (99%)
  local copies, waits for them, and re-layouts  0.62 us (1%)
    pallas_call x1, Pallas kernels, body(): pl.pallas_call(kernel, out_shape=pltpu.VMEM(cycles.shape, F32), in_specs=...  48.9 us

profile of v8, /device:TPU:1, one launch (start us, length us, event | category | flops | bytes accessed | tf_op | source)
XLA Modules:
  0.0 49.5 jit_solution(8612963977692837885)
XLA Ops:
  0.0 48.9 %shard_map.73 = f32[2,32,128]{2,1,0:T(8,128)S(1)} custom-call(f32[2,32,128]{2,1,0:T(8,128)} %cycles_hbm.1, f32[2,32,12288]{2,1,0:T(8,128)} %legendre_hbm.1, f32[1,32]{1,0:T(1,128)} %bitcast.3, f32[8,8,768]{2,1,0:T(8,128)} %bitcast.2, s32[2,64]{1,0:T(2,128)} %hit_hbm.1, f32[2,64,128]{2,1,0:T(8,128)} %flux_hbm.1, s32[2]{0:T(128)} %order_hbm.1), custom_call_target="tpu_custom_call" | custom-call | tf_op jit(solution)/shard_map/pallas_call | solution.py:322
  48.9 0.6 %copy.9 = f32[2,32,128]{2,1,0:T(8,128)} copy(f32[2,32,128]{2,1,0:T(8,128)S(1)} %shard_map.73) | data formatting | bytes 65536
